TPU v7x, 128 devices: a whole 4x4x4 slice. The times are simulated.
128 devices in a mesh: group: 16 (over y, z_hi, core), ctx: 8 (over x, z_lo).
Axes of the slice: x: 4, y: 4, z: 4 (z_hi: 2, z_lo: 2; z = z_hi * 2 + z_lo), core: 2. Of those that a mesh axis runs over, the one named last changes fastest.
Arguments:
- query: bfloat16 [16, 4, 32, 8192], P('group', None, None, 'ctx'), may hold values from -160 to 160
- cache_keys: bfloat16 [16, 4, 4096, 1024], P('group', None, 'ctx'), may hold values from -6 to 6
- cache_values: bfloat16 [16, 4, 4096, 1024], P('group', None, 'ctx'), may hold values from -6 to 6
- new_keys: bfloat16 [16, 4, 32, 1024], P('group', None, 'ctx'), may hold values from -6 to 6
- new_values: bfloat16 [16, 4, 32, 1024], P('group', None, 'ctx'), may hold values from -6 to 6
- masks: int32 [3], replicated, may hold values from 1 to 15
- movers: int32 [3, 16], replicated, may hold values from 0 to 3
- block_lists: int32 [3, 16, 4], replicated, may hold values from 0 to 3, as said below
- lengths: int32 [16, 4], replicated, may hold values from 1 to 4096
Outputs:
- attended: bfloat16 [16, 4, 32, 8192], P('group', None, None, 'ctx')
- keys_after: bfloat16 [16, 4, 4096, 1024], P('group', None, 'ctx')
- values_after: bfloat16 [16, 4, 4096, 1024], P('group', None, 'ctx')
Inputs may be any that keep to these rules, and one draw needn't show every extreme that they name: `block_lists`: each row is a permutation of the 4 blocks.
All inputs are finite; a program needn't handle non-finite values.
Results may differ from a plain program's by a relative error of at most 0.005.
Values may be sent and summed in bfloat16 or wider, within the bound.
A program may use at most 192 MiB of HBM per device.

v0:
```python
import jax
import jax.numpy as jnp
from jax import lax
from jax.sharding import PartitionSpec as P

HD = 128
NEW = 32
MATCHINGS = 3
BLOCK = 128


def swapped_2(block, axis, stride):
    count = lax.axis_size(axis)
    route = []
    for low in range(count):
        high = low | 1 << stride
        if high != low and high < count:
            route += [(low, high), (high, low)]
    return lax.ppermute(block, axis, route)


def merged_2(value, axis, join):
    pieces = jax.tree.map(lambda part: lax.all_gather(part, axis), value)
    head = jax.tree.map(lambda part: part[0], pieces)
    tail = jax.tree.map(lambda part: part[1:], pieces)
    so_far, _ = lax.scan(lambda so_far, share: (join(so_far, share), None), head, tail)
    return so_far


def route_blocks(payload, mask_value, groups):
    current = payload
    for bit in range(groups.bit_length() - 1):
        swapped = swapped_2(current, "group", bit)
        flag = jnp.bitwise_and(jnp.right_shift(mask_value, bit), 1) == 1
        current = jnp.where(flag, swapped, current)
    return current


def join_partials(left, right):
    peak = jnp.maximum(left[0], right[0])
    left_factor = jnp.exp(left[0] - peak)
    right_factor = jnp.exp(right[0] - peak)
    rows, tokens, heads = peak.shape
    left_out = left[2].reshape(rows, tokens, heads, -1) * left_factor[..., None]
    right_out = right[2].reshape(rows, tokens, heads, -1) * right_factor[..., None]
    summed = (left_out + right_out).reshape(left[2].shape)
    return (peak, left[1] * left_factor + right[1] * right_factor, summed)


def shards(
    query, cache_keys, cache_values, new_keys, new_values, masks, movers, block_lists, lengths
):
    groups = lax.axis_size("group")
    width = lax.axis_size("ctx")
    here = lax.axis_index("group")
    place = lax.axis_index("ctx")
    keys = cache_keys[0]
    values = cache_values[0]
    segment = keys.shape[1]
    features = keys.shape[2]
    nblocks = segment // BLOCK
    moving = block_lists.shape[2]
    every = jnp.arange(groups, dtype=jnp.int32)
    counts = lengths
    for step in range(MATCHINGS):
        mask_value = masks[step]
        partner = jnp.bitwise_xor(every, mask_value)
        slots = movers[step]
        slot = slots[here]
        chosen = block_lists[step, here]
        key_rows = lax.dynamic_index_in_dim(keys, slot, 0, keepdims=False).reshape(
            nblocks, BLOCK, features
        )
        value_rows = lax.dynamic_index_in_dim(values, slot, 0, keepdims=False).reshape(
            nblocks, BLOCK, features
        )
        payload = jnp.stack(
            [
                jnp.take(key_rows, chosen, axis=0).reshape(moving * BLOCK, features),
                jnp.take(value_rows, chosen, axis=0).reshape(moving * BLOCK, features),
            ]
        )
        arrived = route_blocks(payload, mask_value, groups).reshape(2, moving, BLOCK, features)
        key_rows = key_rows.at[chosen].set(arrived[0])
        value_rows = value_rows.at[chosen].set(arrived[1])
        keys = lax.dynamic_update_index_in_dim(keys, key_rows.reshape(segment, features), slot, 0)
        values = lax.dynamic_update_index_in_dim(
            values, value_rows.reshape(segment, features), slot, 0
        )
        counts = counts.at[every, slots].set(counts[partner, slots[partner]])
    own_counts = counts[here]
    gathered = lax.all_gather(query[0], "ctx", axis=2, tiled=True)
    heads = gathered.shape[2] // HD
    kv_heads = features // HD
    ratio = heads // kv_heads
    local_new = new_keys.shape[2]
    scale = 1.0 / HD**0.5
    positions = place * segment + jnp.arange(segment, dtype=jnp.int32)
    new_index = place * local_new + jnp.arange(local_new, dtype=jnp.int32)
    token_index = jnp.arange(NEW, dtype=jnp.int32)
    valid_new = new_index[None, :] <= token_index[:, None]

    def partial_attention(args):
        asked, key_block, value_block, fresh_keys, fresh_values, count = args
        heads_q = asked.reshape(NEW, kv_heads, ratio, HD)
        older = (
            jnp.einsum(
                "tkgd,skd->kgts",
                heads_q,
                key_block.reshape(segment, kv_heads, HD),
                preferred_element_type=jnp.float32,
            )
            * scale
        )
        newer = (
            jnp.einsum(
                "tkgd,skd->kgts",
                heads_q,
                fresh_keys.reshape(local_new, kv_heads, HD),
                preferred_element_type=jnp.float32,
            )
            * scale
        )
        valid_old = (positions < count)[None, None, None, :]
        older = jnp.where(valid_old, older, -1e30)
        newer = jnp.where(valid_new[None, None], newer, -1e30)
        top = jnp.maximum(jnp.max(older, axis=-1), jnp.max(newer, axis=-1))
        exp_old = jnp.where(valid_old, jnp.exp(older - top[..., None]), 0.0)
        exp_new = jnp.where(valid_new[None, None], jnp.exp(newer - top[..., None]), 0.0)
        total = jnp.sum(exp_old, axis=-1) + jnp.sum(exp_new, axis=-1)
        summed = jnp.einsum(
            "kgts,skd->tkgd",
            exp_old.astype(jnp.bfloat16),
            value_block.reshape(segment, kv_heads, HD),
            preferred_element_type=jnp.float32,
        )
        summed = summed + jnp.einsum(
            "kgts,skd->tkgd",
            exp_new.astype(jnp.bfloat16),
            fresh_values.reshape(local_new, kv_heads, HD),
            preferred_element_type=jnp.float32,
        )
        top_rows = jnp.transpose(top, (2, 0, 1)).reshape(NEW, heads)
        total_rows = jnp.transpose(total, (2, 0, 1)).reshape(NEW, heads)
        return (top_rows, total_rows, summed.reshape(NEW, heads * HD))

    top, total, summed = lax.map(
        partial_attention, (gathered, keys, values, new_keys[0], new_values[0], own_counts)
    )
    own = heads // width
    requests = summed.shape[0]
    merged = merged_2((top, total, summed), "ctx", join_partials)
    denom = lax.dynamic_slice_in_dim(merged[1], place * own, own, 2)
    numer = lax.dynamic_slice_in_dim(merged[2], place * own * HD, own * HD, 2)
    attended = (numer.reshape(requests, NEW, own, HD) / denom[..., None]).reshape(
        requests, NEW, own * HD
    )
    return (attended.astype(jnp.bfloat16)[None], keys[None], values[None])


def solution(mesh):
    placed = (
        P("group", None, None, "ctx"),
        P("group", None, "ctx", None),
        P("group", None, "ctx", None),
        P("group", None, "ctx", None),
        P("group", None, "ctx", None),
        P(),
        P(),
        P(),
        P(),
    )
    return jax.shard_map(
        shards,
        mesh=mesh,
        in_specs=placed,
        out_specs=(
            P("group", None, None, "ctx"),
            P("group", None, "ctx", None),
            P("group", None, "ctx", None),
        ),
        check_vma=False,
    )
```

profile of v0, /device:TPU:0, one launch (start us, length us, event | category | flops | bytes accessed | tf_op | source)
XLA Modules:
  0.0 1484.0 jit_solution(5700261324864411184)
XLA Ops:
  37.5 45.6 %collective-permute-done.1 = bf16[2,512,1024]{2,1,0:T(8,128)(2,1)} collective-permute-done((bf16[2,512,1024]{2,1,0:T(8,128)(2,1)}, bf16[2,512,1024]{2,1,0:T(8,128)(2,1)}, u32[]{:S(2)}, u32[]{:S(2)}) %collective-permute-start.1) | collective-permute-done | bytes 2097184 | tf_op jit(solution)/shard_map/ppermute | solution.py:19
  88.7 45.1 %collective-permute-done.2 = bf16[2,512,1024]{2,1,0:T(8,128)(2,1)} collective-permute-done((bf16[2,512,1024]{2,1,0:T(8,128)(2,1)}, bf16[2,512,1024]{2,1,0:T(8,128)(2,1)}, u32[]{:S(2)}, u32[]{:S(2)}) %collective-permute-start.2) | collective-permute-done | bytes 2097184 | tf_op jit(solution)/shard_map/ppermute | solution.py:19
  143.5 41.6 %collective-permute-done.3 = bf16[2,512,1024]{2,1,0:T(8,128)(2,1)} collective-permute-done((bf16[2,512,1024]{2,1,0:T(8,128)(2,1)}, bf16[2,512,1024]{2,1,0:T(8,128)(2,1)}, u32[]{:S(2)}, u32[]{:S(2)}) %collective-permute-start.3) | collective-permute-done | bytes 2097184 | tf_op jit(solution)/shard_map/ppermute | solution.py:19
  212.7 46.2 %collective-permute-done.5 = bf16[2,512,1024]{2,1,0:T(8,128)(2,1)} collective-permute-done((bf16[2,512,1024]{2,1,0:T(8,128)(2,1)}, bf16[2,512,1024]{2,1,0:T(8,128)(2,1)}, u32[]{:S(2)}, u32[]{:S(2)}) %collective-permute-start.5) | collective-permute-done | bytes 2097184 | tf_op jit(solution)/shard_map/ppermute | solution.py:19
  264.5 45.0 %collective-permute-done.6 = bf16[2,512,1024]{2,1,0:T(8,128)(2,1)} collective-permute-done((bf16[2,512,1024]{2,1,0:T(8,128)(2,1)}, bf16[2,512,1024]{2,1,0:T(8,128)(2,1)}, u32[]{:S(2)}, u32[]{:S(2)}) %collective-permute-start.6) | collective-permute-done | bytes 2097184 | tf_op jit(solution)/shard_map/ppermute | solution.py:19
  318.4 42.0 %collective-permute-done.7 = bf16[2,512,1024]{2,1,0:T(8,128)(2,1)} collective-permute-done((bf16[2,512,1024]{2,1,0:T(8,128)(2,1)}, bf16[2,512,1024]{2,1,0:T(8,128)(2,1)}, u32[]{:S(2)}, u32[]{:S(2)}) %collective-permute-start.7) | collective-permute-done | bytes 2097184 | tf_op jit(solution)/shard_map/ppermute | solution.py:19
  388.1 46.2 %collective-permute-done.9 = bf16[2,512,1024]{2,1,0:T(8,128)(2,1)} collective-permute-done((bf16[2,512,1024]{2,1,0:T(8,128)(2,1)}, bf16[2,512,1024]{2,1,0:T(8,128)(2,1)}, u32[]{:S(2)}, u32[]{:S(2)}) %collective-permute-start.9) | collective-permute-done | bytes 2097184 | tf_op jit(solution)/shard_map/ppermute | solution.py:19
  440.0 44.9 %collective-permute-done.10 = bf16[2,512,1024]{2,1,0:T(8,128)(2,1)} collective-permute-done((bf16[2,512,1024]{2,1,0:T(8,128)(2,1)}, bf16[2,512,1024]{2,1,0:T(8,128)(2,1)}, u32[]{:S(2)}, u32[]{:S(2)}) %collective-permute-start.10) | collective-permute-done | bytes 2097184 | tf_op jit(solution)/shard_map/ppermute | solution.py:19
  503.8 31.9 %collective-permute-done.11 = bf16[2,512,1024]{2,1,0:T(8,128)(2,1)} collective-permute-done((bf16[2,512,1024]{2,1,0:T(8,128)(2,1)}, bf16[2,512,1024]{2,1,0:T(8,128)(2,1)}, u32[]{:S(2)}, u32[]{:S(2)}) %collective-permute-start.11) | collective-permute-done | bytes 2097184 | tf_op jit(solution)/shard_map/ppermute | solution.py:19
  543.5 79.1 %while.30 = (s32[]{:T(128)}, f32[4,32,64]{2,1,0:T(8,128)S(1)}, f32[4,32,64]{2,1,0:T(8,128)S(1)}, f32[4,32,8192]{2,1,0:T(8,128)}, s32[4]{0:T(128)S(1)}, /*index=5...) while((s32[]{:T(128)}, f32[4,32,64]{2,1,0:T(8,128)S(1)}, ...), condition=%wide.region_14.16_spmd.clone, body=%wide.region_9.0_spmd.clone.sunk | while | flops 555029632 | bytes 35983536 | solution.py:147
  622.7 74.0 %all-gather.1 = f32[32,32,64]{2,1,0:T(8,128)S(1)} all-gather(f32[4,32,64]{2,1,0:T(8,128)S(1)} %get-tuple-element.106), channel_id=3, replica_groups=mesh['group'=16,'ctx'=8] {'ctx'}, dimensions={0}, use_global_device_ids=true | all-gather | bytes 294912 | tf_op jit(solution)/shard_map/all_gather | solution.py:23
  696.7 49.9 %all-gather.2 = f32[32,32,64]{2,1,0:T(8,128)S(1)} all-gather(f32[4,32,64]{2,1,0:T(8,128)S(1)} %get-tuple-element.107), channel_id=4, replica_groups=mesh['group'=16,'ctx'=8] {'ctx'}, dimensions={0}, use_global_device_ids=true | all-gather | bytes 294912 | tf_op jit(solution)/shard_map/all_gather | solution.py:23
  746.7 533.4 %all-gather.9.cloned.1.call-done = f32[32,32,8192]{2,1,0:T(8,128)} async-done(((f32[4,32,8192]{2,1,0:T(8,128)}), f32[32,32,8192]{2,1,0:T(8,128)}) %all-gather.9.cloned.1.call-update) | async-done | bytes 33554448 | tf_op jit(solution)/shard_map/all_gather | solution.py:23
  1280.1 21.4 %slice.125 = f32[28,32,8192]{2,1,0:T(8,128)} slice(f32[32,32,8192]{2,1,0:T(8,128)} %all-gather.9.cloned.1.call-done), slice={[4:32], [0:32], [0:8192]} | slice | bytes 58720256 | tf_op jit(solution)/shard_map/slice | solution.py:25
  1306.1 168.8 %while.29 = (s32[]{:T(128)}, f32[4,32,64]{2,1,0:T(8,128)S(1)}, f32[4,32,64]{2,1,0:T(8,128)S(1)}, f32[4,32,8192]{2,1,0:T(8,128)}, f32[7,4,32,64]{3,2,1,0:T(8,128)...) while((s32[]{:T(128)}, f32[4,32,64]{2,1,0:T(8,128)S(1)}, ...), condition=%wide.region_16.18_spmd, body=%wide.region_15.17_spmd.sunk | while | flops 3194882 | bytes 46465116 | solution.py:26
  1308.7 4.9 mul.97
  1316.2 5.0 mul.99
  1321.2 9.0 fusion.89
  1332.8 4.9 mul.97
  1340.4 5.0 mul.99
  1345.3 9.0 fusion.89
  1357.0 4.9 mul.97
  1364.5 5.0 mul.99
  1369.4 9.0 fusion.89
  1388.6 5.0 mul.99
  1393.6 9.0 fusion.89
  1412.7 5.0 mul.99
  1417.7 9.0 fusion.89
  1436.8 5.0 mul.99
  1441.8 9.0 fusion.89
  1460.9 5.0 mul.99
  1465.9 9.0 fusion.89
  (245 shorter events, 276.0 us)
Async XLA Ops:
  7.2 536.4 %all-gather.7.cloned.1.call-start = ((), (), s32[]{:S(2)}) async-start(), calls=%async_computation | async-start | bytes 2359296 | tf_op jit(solution)/shard_map/all_gather | solution.py:92
  7.2 4.8 copy-start.3
  12.0 2.0 copy-start.7
  12.0 2.0 copy-start.4
  12.0 2.3 copy-start.6
  23.8 1.6 copy-start
  23.9 1.6 copy-start.5
  25.5 4.5 collective-permute-start
  32.8 50.2 %collective-permute-start.1 = (bf16[2,512,1024]{2,1,0:T(8,128)(2,1)}, bf16[2,512,1024]{2,1,0:T(8,128)(2,1)}, u32[]{:S(2)}, u32[]{:S(2)}) collective-permute-start(bf16[2,512,1024]{2,1,0:T(8,128)(2,1)} %broadcast_select_fusion.8), channel_id=1, source_target_pairs={{0,16},{16,0},{8,24},{24,8},{32,48},{48,32},{40,56},{56,40},{64,80... | collective-permute-start | bytes 6291464 | tf_op jit(solution)/shard_map/ppermute | solution.py:19
  86.5 47.4 %collective-permute-start.2 = (bf16[2,512,1024]{2,1,0:T(8,128)(2,1)}, bf16[2,512,1024]{2,1,0:T(8,128)(2,1)}, u32[]{:S(2)}, u32[]{:S(2)}) collective-permute-start(bf16[2,512,1024]{2,1,0:T(8,128)(2,1)} %broadcast_select_fusion.9), channel_id=1, source_target_pairs={{0,32},{32,0},{8,40},{40,8},{16,48},{48,16},{24,56},{56,24},{64,96... | collective-permute-start | bytes 6291464 | tf_op jit(solution)/shard_map/ppermute | solution.py:19
  137.0 48.1 %collective-permute-start.3 = (bf16[2,512,1024]{2,1,0:T(8,128)(2,1)}, bf16[2,512,1024]{2,1,0:T(8,128)(2,1)}, u32[]{:S(2)}, u32[]{:S(2)}) collective-permute-start(bf16[2,512,1024]{2,1,0:T(8,128)(2,1)} %broadcast_select_fusion.10), channel_id=1, source_target_pairs={{0,64},{64,0},{8,72},{72,8},{16,80},{80,16},{24,88},{88,24},{32,96... | collective-permute-start | bytes 6291464 | tf_op jit(solution)/shard_map/ppermute | solution.py:19
  200.5 1.6 copy-start.2
  202.1 4.5 collective-permute-start.4
  209.4 49.5 %collective-permute-start.5 = (bf16[2,512,1024]{2,1,0:T(8,128)(2,1)}, bf16[2,512,1024]{2,1,0:T(8,128)(2,1)}, u32[]{:S(2)}, u32[]{:S(2)}) collective-permute-start(bf16[2,512,1024]{2,1,0:T(8,128)(2,1)} %broadcast_select_fusion.4), channel_id=1, source_target_pairs={{0,16},{16,0},{8,24},{24,8},{32,48},{48,32},{40,56},{56,40},{64,80... | collective-permute-start | bytes 6291464 | tf_op jit(solution)/shard_map/ppermute | solution.py:19
  262.4 47.1 %collective-permute-start.6 = (bf16[2,512,1024]{2,1,0:T(8,128)(2,1)}, bf16[2,512,1024]{2,1,0:T(8,128)(2,1)}, u32[]{:S(2)}, u32[]{:S(2)}) collective-permute-start(bf16[2,512,1024]{2,1,0:T(8,128)(2,1)} %broadcast_select_fusion.5), channel_id=1, source_target_pairs={{0,32},{32,0},{8,40},{40,8},{16,48},{48,16},{24,56},{56,24},{64,96... | collective-permute-start | bytes 6291464 | tf_op jit(solution)/shard_map/ppermute | solution.py:19
  312.6 47.8 %collective-permute-start.7 = (bf16[2,512,1024]{2,1,0:T(8,128)(2,1)}, bf16[2,512,1024]{2,1,0:T(8,128)(2,1)}, u32[]{:S(2)}, u32[]{:S(2)}) collective-permute-start(bf16[2,512,1024]{2,1,0:T(8,128)(2,1)} %broadcast_select_fusion.6), channel_id=1, source_target_pairs={{0,64},{64,0},{8,72},{72,8},{16,80},{80,16},{24,88},{88,24},{32,96... | collective-permute-start | bytes 6291464 | tf_op jit(solution)/shard_map/ppermute | solution.py:19
  375.8 1.6 copy-start.1
  377.5 4.5 collective-permute-start.8
  384.8 49.5 %collective-permute-start.9 = (bf16[2,512,1024]{2,1,0:T(8,128)(2,1)}, bf16[2,512,1024]{2,1,0:T(8,128)(2,1)}, u32[]{:S(2)}, u32[]{:S(2)}) collective-permute-start(bf16[2,512,1024]{2,1,0:T(8,128)(2,1)} %broadcast_select_fusion), channel_id=1, source_target_pairs={{0,16},{16,0},{8,24},{24,8},{32,48},{48,32},{40,56},{56,40},{64,80... | collective-permute-start | bytes 6291464 | tf_op jit(solution)/shard_map/ppermute | solution.py:19
  437.7 47.1 %collective-permute-start.10 = (bf16[2,512,1024]{2,1,0:T(8,128)(2,1)}, bf16[2,512,1024]{2,1,0:T(8,128)(2,1)}, u32[]{:S(2)}, u32[]{:S(2)}) collective-permute-start(bf16[2,512,1024]{2,1,0:T(8,128)(2,1)} %broadcast_select_fusion.1), channel_id=1, source_target_pairs={{0,32},{32,0},{8,40},{40,8},{16,48},{48,16},{24,56},{56,24},{64,96... | collective-permute-start | bytes 6291464 | tf_op jit(solution)/shard_map/ppermute | solution.py:19
  439.3 840.8 %all-gather.9.cloned.1.call-start = ((), (), s32[]{:S(2)}) async-start(), calls=%async_computation.1 | async-start | bytes 37748736 | tf_op jit(solution)/shard_map/all_gather | solution.py:23
  488.0 47.8 %collective-permute-start.11 = (bf16[2,512,1024]{2,1,0:T(8,128)(2,1)}, bf16[2,512,1024]{2,1,0:T(8,128)(2,1)}, u32[]{:S(2)}, u32[]{:S(2)}) collective-permute-start(bf16[2,512,1024]{2,1,0:T(8,128)(2,1)} %broadcast_select_fusion.2), channel_id=1, source_target_pairs={{0,64},{64,0},{8,72},{72,8},{16,80},{80,16},{24,88},{88,24},{32,96... | collective-permute-start | bytes 6291464 | tf_op jit(solution)/shard_map/ppermute | solution.py:19
Sparse Core Ops, SparseCore 0:
  439.4 52.8 all-gather.6
  622.8 657.2 all-gather.8
where the time goes:
time: 1490 us; the launch traced here: 1480 us
  waiting for transfers between devices  933 us (63%)
  local copies, waits for them, and re-layouts  210 us (14%)
  other arithmetic  130 us (9%)
  blocking collectives  124 us (8%)
  matrix products  34.8 us (2%)
  between operations  28 us (2%)
  starting transfers between devices  23.8 us (2%)
    all_gather x1, waiting for transfers between devices, merged_2(): pieces = jax.tree.map(lambda part: lax.all_gather(part, axis), value)  533 us
    ppermute x12, waiting for transfers between devices, swapped_2(): return lax.ppermute(block, axis, route)  399 us
    all_gather x2, blocking collectives, merged_2(): pieces = jax.tree.map(lambda part: lax.all_gather(part, axis), value)  124 us
    add x7, other arithmetic, join_partials(): summed = (left_out + right_out).reshape(left[2].shape)  62.8 us
    mul x14, local copies, waits for them, and re-layouts, join_partials(): left_out = left[2].reshape(rows, tokens, heads, -1) * left_factor[..., None]  52.8 us
    mul x14, local copies, waits for them, and re-layouts, join_partials(): right[2].reshape(rows, tokens, heads, -1) * right_factor[..., None]  52.8 us
    select_n x12, other arithmetic, route_blocks(): current = jnp.where(flag, swapped, current)  33.5 us
  transfers between devices with their start and end apart: 14, of which 13 were waited for; matrix products, arithmetic and copies ran while one was open for 2% of the time, Pallas kernels for 0%

commit v1 on v0

v1 whole, which is shorter than its diff:
```python
import functools
import math

import jax
import jax.numpy as jnp
from jax import lax
from jax.experimental import pallas as pl
from jax.experimental.pallas import tpu as pltpu
from jax.sharding import PartitionSpec as P

HD = 128
NEW = 32
MATCHINGS = 3
BLOCK = 128
GROUPS = 16
WIDTH = 8
SLOTS = 4
SEG = 512
NB = 4
FEATURES = 1024
KVH = 8
GQ = 8
ROWS = GQ * NEW
OWN_NEW = 4
PAD_NEW = 16
MESH = pl.DeviceIdType.MESH
ANY = pl.ANY


def peer_at(place, offset):
    x, z = place // 2, place % 2
    return ((x + offset // 2) % 4) * 2 + (z + offset % 2) % 2


def pack_body(where, keys_ref, values_ref, out_ref):
    out_ref[0, 0] = keys_ref[0]
    out_ref[1, 0] = values_ref[0]


def pack(where, keys, values):
    def spec():
        return pl.BlockSpec((1, BLOCK, FEATURES), lambda j, w: (w[0], w[1 + j], 0))

    return pl.pallas_call(
        pack_body,
        grid_spec=pltpu.PrefetchScalarGridSpec(
            num_scalar_prefetch=1,
            grid=(NB,),
            in_specs=[spec(), spec()],
            out_specs=pl.BlockSpec((2, 1, BLOCK, FEATURES), lambda j, w: (0, j, 0, 0)),
        ),
        out_shape=jax.ShapeDtypeStruct((2, NB, BLOCK, FEATURES), jnp.bfloat16),
        name="pack",
    )(where, keys, values)


def unpack_body(where, arrived_ref, keys_in, values_in, keys_ref, values_ref):
    keys_ref[0] = arrived_ref[0, 0]
    values_ref[0] = arrived_ref[1, 0]


def unpack(where, arrived, keys, values):
    def spec():
        return pl.BlockSpec((1, BLOCK, FEATURES), lambda j, w: (w[0], w[1 + j], 0))

    shape = jax.ShapeDtypeStruct(keys.shape, keys.dtype)
    return pl.pallas_call(
        unpack_body,
        grid_spec=pltpu.PrefetchScalarGridSpec(
            num_scalar_prefetch=1,
            grid=(NB,),
            in_specs=[
                pl.BlockSpec((2, 1, BLOCK, FEATURES), lambda j, w: (0, j, 0, 0)),
                pl.BlockSpec(memory_space=ANY),
                pl.BlockSpec(memory_space=ANY),
            ],
            out_specs=[spec(), spec()],
        ),
        out_shape=[shape, shape],
        input_output_aliases={2: 0, 3: 1},
        name="unpack",
    )(where, arrived, keys, values)


def gather_queries(query):
    parts = [query]
    for offset in range(1, WIDTH):
        route = [(peer_at(me, offset), me) for me in range(WIDTH)]
        parts.append(lax.ppermute(query, "ctx", route))
    return jnp.stack(parts)


def exchange(mask, payload):
    def branch(d):
        route = [(g, g ^ d) for g in range(GROUPS)]
        return lambda block: lax.ppermute(block, "group", route)

    return lax.switch(mask - 1, [branch(d) for d in range(1, GROUPS)], payload)


def attend_body(plan, valid, peers, q_ref, k_ref, v_ref, nk_ref, nv_ref, o_ref, s_ref):
    count = valid[pl.program_id(0)]
    first = peers[WIDTH]
    factor = math.log2(math.e) / math.sqrt(HD)
    q = q_ref[0, 0]
    rows = jnp.concatenate([q[:, g * HD : (g + 1) * HD] for g in range(GQ)], axis=0)
    contract_last = (((1,), (1,)), ((), ()))
    contract_first = (((0,), (0,)), ((), ()))
    older = lax.dot_general(k_ref[0], rows, contract_last, preferred_element_type=jnp.float32)
    newer = lax.dot_general(nk_ref[0], rows, contract_last, preferred_element_type=jnp.float32)
    position = lax.broadcasted_iota(jnp.int32, older.shape, 0)
    valid_old = position < count
    fresh = lax.broadcasted_iota(jnp.int32, newer.shape, 0)
    token = lax.broadcasted_iota(jnp.int32, newer.shape, 1) % NEW
    valid_new = jnp.logical_and(fresh < OWN_NEW, first + fresh <= token)
    older = jnp.where(valid_old, older, -1e30)
    newer = jnp.where(valid_new, newer, -1e30)
    top = jnp.maximum(
        jnp.max(older, axis=0, keepdims=True), jnp.max(newer, axis=0, keepdims=True)
    )
    exp_old = jnp.where(valid_old, jnp.exp2((older - top) * factor), 0.0)
    exp_new = jnp.where(valid_new, jnp.exp2((newer - top) * factor), 0.0)
    total = jnp.sum(exp_old, axis=0, keepdims=True) + jnp.sum(exp_new, axis=0, keepdims=True)
    summed = lax.dot_general(
        v_ref[0], exp_old.astype(jnp.bfloat16), contract_first, preferred_element_type=jnp.float32
    )
    summed += lax.dot_general(
        nv_ref[0], exp_new.astype(jnp.bfloat16), contract_first, preferred_element_type=jnp.float32
    )
    o_ref[0, 0] = summed.astype(jnp.bfloat16)
    row = lax.broadcasted_iota(jnp.int32, (8, ROWS), 0)
    s_ref[0, 0] = jnp.where(row == 0, top, total)


def attend(plan, valid, peers, queries, keys, values, new_keys, new_values):
    n = plan.shape[0]

    def cache():
        return pl.BlockSpec((1, SEG, HD), lambda i, o, p, v, e: (p[i], 0, e[o]))

    def new():
        return pl.BlockSpec((1, PAD_NEW, HD), lambda i, o, p, v, e: (p[i], 0, e[o]))

    return pl.pallas_call(
        attend_body,
        grid_spec=pltpu.PrefetchScalarGridSpec(
            num_scalar_prefetch=3,
            grid=(n, WIDTH),
            in_specs=[
                pl.BlockSpec((1, 1, NEW, GQ * HD), lambda i, o, p, v, e: (o, p[i], 0, 0)),
                cache(),
                cache(),
                new(),
                new(),
            ],
            out_specs=[
                pl.BlockSpec((1, 1, HD, ROWS), lambda i, o, p, v, e: (e[o], i, 0, 0)),
                pl.BlockSpec((1, 1, 8, ROWS), lambda i, o, p, v, e: (e[o], i, 0, 0)),
            ],
        ),
        out_shape=[
            jax.ShapeDtypeStruct((WIDTH, n, HD, ROWS), jnp.bfloat16),
            jax.ShapeDtypeStruct((WIDTH, n, 8, ROWS), jnp.float32),
        ],
        name="attend",
    )(plan, valid, peers, queries, keys, values, new_keys, new_values)


def combine_body(n, o_ref, s_ref, out_ref, o_all, s_all, sem_o, sem_s, arrive_o, arrive_s, local):
    group = lax.axis_index("group")
    place = lax.axis_index("ctx")
    barrier = pltpu.get_barrier_semaphore()
    for offset in range(1, WIDTH):
        pl.semaphore_signal(
            barrier, inc=1, device_id=(group, peer_at(place, offset)), device_id_type=MESH
        )
    own_o = pltpu.make_async_copy(o_ref.at[place], o_all.at[0], local.at[0])
    own_s = pltpu.make_async_copy(s_ref.at[place], s_all.at[0], local.at[1])
    own_o.start()
    own_s.start()
    pl.semaphore_wait(barrier, WIDTH - 1)
    sends = []
    for offset in range(1, WIDTH):
        peer = peer_at(place, offset)
        for src, dst, send, recv in (
            (o_ref, o_all, sem_o, arrive_o),
            (s_ref, s_all, sem_s, arrive_s),
        ):
            copy = pltpu.make_async_remote_copy(
                src_ref=src.at[peer],
                dst_ref=dst.at[offset],
                send_sem=send.at[offset],
                recv_sem=recv.at[offset],
                device_id=(group, peer),
                device_id_type=MESH,
            )
            copy.start()
            sends.append(copy)
    own_o.wait()
    own_s.wait()
    for copy in sends:
        copy.wait()
    factor = math.log2(math.e) / math.sqrt(HD)
    for i in range(n):
        stats = [s_all[offset, i] for offset in range(WIDTH)]
        tops = [part[0:1] for part in stats]
        totals = [part[1:2] for part in stats]
        top = functools.reduce(jnp.maximum, tops)
        scales = [jnp.exp2((part - top) * factor) for part in tops]
        total = sum(a * b for a, b in zip(scales, totals))
        merged = sum(
            o_all[offset, i].astype(jnp.float32) * scales[offset] for offset in range(WIDTH)
        )
        rows = jnp.transpose(merged / total)
        for g in range(GQ):
            out_ref[i, :, g * HD : (g + 1) * HD] = rows[g * NEW : (g + 1) * NEW].astype(
                jnp.bfloat16
            )


def combine(partial, stats):
    n = partial.shape[1]
    dma = pltpu.SemaphoreType.DMA((WIDTH,))
    return pl.pallas_call(
        functools.partial(combine_body, n),
        in_specs=[pl.BlockSpec(memory_space=ANY)] * 2,
        out_specs=pl.BlockSpec(memory_space=pltpu.VMEM),
        out_shape=jax.ShapeDtypeStruct((n, NEW, GQ * HD), jnp.bfloat16),
        scratch_shapes=[
            pltpu.VMEM((WIDTH, n, HD, ROWS), jnp.bfloat16),
            pltpu.VMEM((WIDTH, n, 8, ROWS), jnp.float32),
            dma,
            dma,
            dma,
            dma,
            pltpu.SemaphoreType.DMA((2,)),
        ],
        compiler_params=pltpu.CompilerParams(collective_id=0, has_side_effects=True),
        name="combine",
    )(partial, stats)


def shards(
    query, cache_keys, cache_values, new_keys, new_values, masks, movers, block_lists, lengths
):
    here = lax.axis_index("group")
    place = lax.axis_index("ctx")
    keys = cache_keys[0]
    values = cache_values[0]
    every = jnp.arange(GROUPS, dtype=jnp.int32)
    counts = lengths
    queries = gather_queries(query[0])
    for step in range(MATCHINGS):
        partner = jnp.bitwise_xor(every, masks[step])
        slots = movers[step]
        counts = counts.at[every, slots].set(counts[partner, slots[partner]])
        where = jnp.concatenate([slots[here][None], block_lists[step, here]])
        payload = pack(where, keys, values)
        arrived = exchange(masks[step], payload)
        keys, values = unpack(where, arrived, keys, values)
    valid = jnp.clip(counts[here] - place * SEG, 0, SEG)
    peers = jnp.stack([peer_at(place, offset) for offset in range(WIDTH)] + [place * OWN_NEW])
    peers = peers.astype(jnp.int32)
    pad = ((0, 0), (0, PAD_NEW - OWN_NEW), (0, 0))
    plan = jnp.arange(SLOTS, dtype=jnp.int32)
    partial, stats = attend(
        plan,
        valid[plan],
        peers,
        queries,
        keys,
        values,
        jnp.pad(new_keys[0], pad),
        jnp.pad(new_values[0], pad),
    )
    attended = combine(partial, stats)
    return (attended[None], keys[None], values[None])


def solution(mesh):
    placed = (
        P("group", None, None, "ctx"),
        P("group", None, "ctx", None),
        P("group", None, "ctx", None),
        P("group", None, "ctx", None),
        P("group", None, "ctx", None),
        P(),
        P(),
        P(),
        P(),
    )
    return jax.shard_map(
        shards,
        mesh=mesh,
        in_specs=placed,
        out_specs=(
            P("group", None, None, "ctx"),
            P("group", None, "ctx", None),
            P("group", None, "ctx", None),
        ),
        check_vma=False,
    )
```

time: 1490 us -> 292 us (0.20)
  waiting for transfers between devices: 933 us -> 152 us
  local copies, waits for them, and re-layouts: 210 us -> 24.7 us
  blocking collectives: 124 us -> 0 us
  other arithmetic: 130 us -> 7.1 us
  Pallas kernels: 0 us -> 84.4 us
  matrix products: 34.8 us -> 0 us
  between operations: 28 us -> 2.96 us
    all_gather x2 -> x0, waiting for transfers between devices: 533 us -> none  [the longest x1 533 us: merged_2(): pieces = jax.tree.map(lambda part: lax.all_gather(part, axis), value)]
    ppermute x12 -> x10, waiting for transfers between devices: 399 us -> 152 us  [the longest x3 141 us: branch(): return lambda block: lax.ppermute(block, 'group', route)]
    all_gather x2 -> x0, blocking collectives: 124 us -> none  [merged_2(): pieces = jax.tree.map(lambda part: lax.all_gather(part, axis), value)]
    mul x28 -> x0, local copies, waits for them, and re-layouts: 106 us -> none  [the longest x14 52.8 us: join_partials(): left_out = left[2].reshape(rows, tokens, heads, -1) * left_factor[..., None]]
    pallas_call x0 -> x8, Pallas kernels: none -> 84.4 us  [the longest x1 31.9 us: combine(): pl.pallas_call(functools.partial(combine_body, n), in_specs=[pl.BlockSpec...]
    add x15 -> x0, other arithmetic: 63.2 us -> none  [the longest x7 62.8 us: join_partials(): summed = (left_out + right_out).reshape(left[2].shape)]
    select_n x19 -> x0, other arithmetic: 38.9 us -> none  [the longest x12 33.5 us: route_blocks(): current = jnp.where(flag, swapped, current)]
    dot_general x16 -> x0, matrix products: 34.8 us -> none  [the longest x4 13 us: partial_attention(): jnp.einsum('kgts,skd->tkgd', exp_old.astype(jnp.bfloat16), value_block.re...]
  transfers between devices with their start and end apart: 14 -> 10, of which waited for: 13 -> 5; matrix products, arithmetic and copies ran while one was open for 2% -> 8% of each run, Pallas kernels for 0% -> 8%
where the time goes in v1:
time: 292 us; the launch traced here: 286 us
  waiting for transfers between devices  152 us (52%)
  Pallas kernels  84.4 us (29%)
  local copies, waits for them, and re-layouts  24.7 us (8%)
  starting transfers between devices  15.2 us (5%)
  other arithmetic  7.1 us (2%)
  between operations  2.96 us (1%)
    ppermute x3, waiting for transfers between devices, branch(): return lambda block: lax.ppermute(block, 'group', route)  141 us
    pallas_call x1, Pallas kernels, combine(): pl.pallas_call(functools.partial(combine_body, n), in_specs=[pl.BlockSpec...  31.9 us
    pallas_call x1, Pallas kernels, attend(): pl.pallas_call(attend_body, grid_spec=pltpu.PrefetchScalarGridSpec(num_sc...  29.6 us
    pallas_call x3, Pallas kernels, unpack(): pl.pallas_call(unpack_body, grid_spec=pltpu.PrefetchScalarGridSpec(num_sc...  13.5 us
    ppermute x7, waiting for transfers between devices, gather_queries(): parts.append(lax.ppermute(query, 'ctx', route))  11.1 us
    ppermute x7, starting transfers between devices, gather_queries(): parts.append(lax.ppermute(query, 'ctx', route))  10.8 us
    unnamed x29, local copies, waits for them, and re-layouts  10.4 us
    pallas_call x3, Pallas kernels, pack(): pl.pallas_call(pack_body, grid_spec=pltpu.PrefetchScalarGridSpec(num_scal...  9.41 us
  transfers between devices with their start and end apart: 10, of which 5 were waited for; matrix products, arithmetic and copies ran while one was open for 8% of the time, Pallas kernels for 8%

profile of v1, /device:TPU:0, one launch (start us, length us, event | category | flops | bytes accessed | tf_op | source)
XLA Modules:
  0.0 286.4 jit_solution(17234406022093601202)
XLA Ops:
  0.6 4.8 %copy.83 = bf16[1,4,512,1024]{3,2,1,0:T(8,128)(2,1)} copy(bf16[1,4,512,1024]{3,2,1,0:T(8,128)(2,1)} %param.55) | data formatting | bytes 8388608
  5.5 2.0 copy.84
  7.5 2.0 collective-permute-start.45
  9.5 2.8 collective-permute-start.46
  14.6 1.2 pad_add_fusion.2.where
  16.4 3.1 %pack.3 = bf16[2,4,128,1024]{3,2,1,0:T(8,128)(2,1)S(1)} custom-call(s32[5]{0:T(128)} %pad_add_fusion.2.where, bf16[4,512,1024]{2,1,0:T(8,128)(2,1)} %bitcast.85, bf16[4,512,1024]{2,1,0:T(8,128)(2,1)} %bitcast.88), custom_call_target="tpu_custom_call" | custom-call | tf_op jit(solution)/shard_map/pack/pallas_call | solution.py:44
  19.6 48.0 %conditional.3 = (bf16[2,4,128,1024]{3,2,1,0:T(8,128)(2,1)}) conditional(s32[]{:T(128)} %clamp.13, bf16[2,4,128,1024]{3,2,1,0:T(8,128)(2,1)S(1)} %pack.3, bf16[2,4,128,1024]{3,2,1,0:T(8,128)(2,1)S(1)} %pack.3, bf16[2,4,128,1024]{3,2,1,0:T(8,128)(2,1)S(1)} %pack.3, bf16[2,4,128,1024]{3,2,1,0:T(8,128)(2,1)S(1)} %pack.3, ...), branch_computations={%region_3.0_spmd, %region_4.0_spmd, %region_5.0_spmd, %region_6.0_... | conditional | bytes 8388656 | solution.py:98
  19.8 47.7 %collective-permute-done.4 = bf16[2,4,128,1024]{3,2,1,0:T(8,128)(2,1)} collective-permute-done((bf16[2,4,128,1024]{3,2,1,0:T(8,128)(2,1)S(1)}, bf16[2,4,128,1024]{3,2,1,0:T(8,128)(2,1)}, u32[]{:S(2)}, u32[]{:S(2)}) %collective-permute-start.4) | collective-permute-done | bytes 2097184 | tf_op jit(solution)/shard_map/cond/branch_4_fun/ppermute | solution.py:96
  67.5 4.5 %unpack.3 = (bf16[4,512,1024]{2,1,0:T(8,128)(2,1)}, bf16[4,512,1024]{2,1,0:T(8,128)(2,1)}) custom-call(s32[5]{0:T(128)} %pad_add_fusion.2.where, bf16[2,4,128,1024]{3,2,1,0:T(8,128)(2,1)} %get-tuple-element.138.arrived_ref, bf16[4,512,1024]{2,1,0:T(8,128)(2,1)} %bitcast.86, bf16[4,512,1024]{2,1,0:T(8,128)(2,1)} %bitcast.89), custom_call_target="tpu_custom_call", output_to_operand_aliasing={{0}: (2, {}), {1}: (3, {})} | custom-call | tf_op jit(solution)/shard_map/unpack/pallas_call | solution.py:67
  73.9 1.9 pad_add_fusion
  75.7 3.1 %pack.4 = bf16[2,4,128,1024]{3,2,1,0:T(8,128)(2,1)S(1)} custom-call(s32[5]{0:T(128)} %get-tuple-element.128.where, bf16[4,512,1024]{2,1,0:T(8,128)(2,1)} %get-tuple-element.104.keys_ref.keys_in, bf16[4,512,1024]{2,1,0:T(8,128)(2,1)} %get-tuple-element.105.values_ref.values_in), custom_call_target="tpu_custom_call" | custom-call | tf_op jit(solution)/shard_map/pack/pallas_call | solution.py:44
  78.9 50.1 %conditional.4 = (bf16[2,4,128,1024]{3,2,1,0:T(8,128)(2,1)}) conditional(s32[]{:T(128)} %clamp.12, bf16[2,4,128,1024]{3,2,1,0:T(8,128)(2,1)S(1)} %pack.4, bf16[2,4,128,1024]{3,2,1,0:T(8,128)(2,1)S(1)} %pack.4, bf16[2,4,128,1024]{3,2,1,0:T(8,128)(2,1)S(1)} %pack.4, bf16[2,4,128,1024]{3,2,1,0:T(8,128)(2,1)S(1)} %pack.4, ...), branch_computations={%region_18.0_spmd, %region_19.0_spmd, %region_20.0_spmd, %region_2... | conditional | bytes 8388656 | solution.py:98
  78.9 4.0 %collective-permute-start.16 = (bf16[2,4,128,1024]{3,2,1,0:T(8,128)(2,1)S(1)}, bf16[2,4,128,1024]{3,2,1,0:T(8,128)(2,1)}, u32[]{:S(2)}, u32[]{:S(2)}) collective-permute-start(bf16[2,4,128,1024]{3,2,1,0:T(8,128)(2,1)S(1)} %param.16), channel_id=1, source_target_pairs={{0,16},{8,24},{16,0},{24,8},{32,48},{40,56},{48,32},{56,40},{64,80... | collective-permute-start | bytes 6291464 | tf_op jit(solution)/shard_map/cond/branch_1_fun/ppermute | solution.py:96
  82.9 46.0 %collective-permute-done.16 = bf16[2,4,128,1024]{3,2,1,0:T(8,128)(2,1)} collective-permute-done((bf16[2,4,128,1024]{3,2,1,0:T(8,128)(2,1)S(1)}, bf16[2,4,128,1024]{3,2,1,0:T(8,128)(2,1)}, u32[]{:S(2)}, u32[]{:S(2)}) %collective-permute-start.16) | collective-permute-done | bytes 2097184 | tf_op jit(solution)/shard_map/cond/branch_1_fun/ppermute | solution.py:96
  128.9 4.5 %unpack.4 = (bf16[4,512,1024]{2,1,0:T(8,128)(2,1)}, bf16[4,512,1024]{2,1,0:T(8,128)(2,1)}) custom-call(s32[5]{0:T(128)} %get-tuple-element.128.where, bf16[2,4,128,1024]{3,2,1,0:T(8,128)(2,1)} %get-tuple-element.139.arrived_ref, bf16[4,512,1024]{2,1,0:T(8,128)(2,1)} %get-tuple-element.104.keys_ref.keys_in, ...), custom_call_target="tpu_custom_call", output_to_operand_aliasing={{0}: (2, {}), {1}: (3, {})} | custom-call | tf_op jit(solution)/shard_map/unpack/pallas_call | solution.py:67
  134.0 3.1 %pack.5 = bf16[2,4,128,1024]{3,2,1,0:T(8,128)(2,1)S(1)} custom-call(s32[5]{0:T(128)} %get-tuple-element.127.where, bf16[4,512,1024]{2,1,0:T(8,128)(2,1)} %get-tuple-element.106.keys_ref.keys_in, bf16[4,512,1024]{2,1,0:T(8,128)(2,1)} %get-tuple-element.107.values_ref.values_in), custom_call_target="tpu_custom_call" | custom-call | tf_op jit(solution)/shard_map/pack/pallas_call | solution.py:44
  137.2 47.3 %conditional.5 = (bf16[2,4,128,1024]{3,2,1,0:T(8,128)(2,1)}) conditional(s32[]{:T(128)} %clamp.11, bf16[2,4,128,1024]{3,2,1,0:T(8,128)(2,1)S(1)} %pack.5, bf16[2,4,128,1024]{3,2,1,0:T(8,128)(2,1)S(1)} %pack.5, bf16[2,4,128,1024]{3,2,1,0:T(8,128)(2,1)S(1)} %pack.5, bf16[2,4,128,1024]{3,2,1,0:T(8,128)(2,1)S(1)} %pack.5, ...), branch_computations={%region_33.0_spmd, %region_34.0_spmd, %region_35.0_spmd, %region_3... | conditional | bytes 8388656 | solution.py:98
  137.3 47.2 %collective-permute-done.33 = bf16[2,4,128,1024]{3,2,1,0:T(8,128)(2,1)} collective-permute-done((bf16[2,4,128,1024]{3,2,1,0:T(8,128)(2,1)S(1)}, bf16[2,4,128,1024]{3,2,1,0:T(8,128)(2,1)}, u32[]{:S(2)}, u32[]{:S(2)}) %collective-permute-start.33) | collective-permute-done | bytes 2097184 | tf_op jit(solution)/shard_map/cond/branch_3_fun/ppermute | solution.py:96
  184.5 3.5 %collective-permute-start.49 = (bf16[4,32,1024]{2,1,0:T(8,128)(2,1)S(1)}, bf16[4,32,1024]{2,1,0:T(8,128)(2,1)}, u32[]{:S(2)}, u32[]{:S(2)}) collective-permute-start(bf16[4,32,1024]{2,1,0:T(8,128)(2,1)S(1)} %bitcast.96), channel_id=1, source_target_pairs={{5,0},{4,1},{7,2},{6,3},{1,4},{0,5},{3,6},{2,7},{13,8},{12,9},{15,... | collective-permute-start | bytes 786440 | tf_op jit(solution)/shard_map/ppermute | solution.py:89
  192.6 1.3 fusion.13
  194.0 4.6 %unpack.5 = (bf16[4,512,1024]{2,1,0:T(8,128)(2,1)}, bf16[4,512,1024]{2,1,0:T(8,128)(2,1)}) custom-call(s32[5]{0:T(128)} %get-tuple-element.127.where, bf16[2,4,128,1024]{3,2,1,0:T(8,128)(2,1)} %get-tuple-element.140.arrived_ref, bf16[4,512,1024]{2,1,0:T(8,128)(2,1)} %get-tuple-element.106.keys_ref.keys_in, ...), custom_call_target="tpu_custom_call", output_to_operand_aliasing={{0}: (2, {}), {1}: (3, {})} | custom-call | tf_op jit(solution)/shard_map/unpack/pallas_call | solution.py:67
  200.7 1.3 scatter_fusion
  202.6 1.3 scatter_fusion.1
  204.6 1.3 scatter_fusion.2
  206.1 1.2 gather_fusion.6
  207.9 1.2 collective-permute-start.50
  209.8 1.0 bitcast_dynamic-update-slice_fusion.2
  210.8 7.5 %collective-permute-done.50 = bf16[4,32,1024]{2,1,0:T(8,128)(2,1)S(1)} collective-permute-done((bf16[4,32,1024]{2,1,0:T(8,128)(2,1)S(1)}, bf16[4,32,1024]{2,1,0:T(8,128)(2,1)S(1)}, u32[]{:S(2)}, u32[]{:S(2)}) %collective-permute-start.50) | collective-permute-done | bytes 262176 | tf_op jit(solution)/shard_map/ppermute | solution.py:89
  218.3 3.5 %collective-permute-done.51 = bf16[4,32,1024]{2,1,0:T(8,128)(2,1)S(1)} collective-permute-done((bf16[4,32,1024]{2,1,0:T(8,128)(2,1)S(1)}, bf16[4,32,1024]{2,1,0:T(8,128)(2,1)S(1)}, u32[]{:S(2)}, u32[]{:S(2)}) %collective-permute-start.51) | collective-permute-done | bytes 262176 | tf_op jit(solution)/shard_map/ppermute | solution.py:89
  223.2 29.6 %attend.1 = (bf16[8,4,128,256]{3,2,1,0:T(8,128)(2,1)}, f32[8,4,8,256]{3,2,1,0:T(8,128)}) custom-call(s32[4]{0:T(128)} %iota.23.plan, s32[4]{0:T(128)} %gather_fusion.6, s32[9]{0:T(128)} %stack.63.peers, bf16[8,4,32,1024]{3,2,1,0:T(8,128)(2,1)} %copy-done.1, bf16[4,512,1024]{2,1,0:T(8,128)(2,1)} %get-tuple-element.108.k_ref, ...), custom_call_target="tpu_custom_call" | custom-call | tf_op jit(solution)/shard_map/attend/pallas_call | solution.py:144
  252.8 31.9 %combine.1 = bf16[4,32,1024]{2,1,0:T(8,128)(2,1)} custom-call(bf16[8,4,128,256]{3,2,1,0:T(8,128)(2,1)} %get-tuple-element.110.o_ref, f32[8,4,8,256]{3,2,1,0:T(8,128)} %get-tuple-element.111.s_ref), custom_call_target="tpu_custom_call" | custom-call | tf_op jit(solution)/shard_map/combine/pallas_call | solution.py:224
  284.8 1.7 copy.86
  (62 shorter events, 14.7 us)
Async XLA Ops:
  0.6 4.8 %copy-start = (bf16[1,4,512,1024]{3,2,1,0:T(8,128)(2,1)S(1)}, bf16[1,4,512,1024]{3,2,1,0:T(8,128)(2,1)}, u32[]{:S(2)}) copy-start(bf16[1,4,512,1024]{3,2,1,0:T(8,128)(2,1)} %param.56) | copy-start | bytes 12582916
  5.5 2.1 copy-start.8
  5.5 2.1 copy-start.2
  5.5 7.7 %copy-start.7 = (s32[3,16]{1,0:T(4,128)S(1)}, s32[3,16]{1,0:T(4,128)}, u32[]{:S(2)}) copy-start(s32[3,16]{1,0:T(4,128)} %param.60) | copy-start | bytes 580
  5.5 8.3 %copy-start.5 = (s32[3,16,4]{1,2,0:T(4,128)S(1)}, s32[3,16,4]{1,2,0:T(4,128)}, u32[]{:S(2)}) copy-start(s32[3,16,4]{1,2,0:T(4,128)} %param.61) | copy-start | bytes 2308
  5.5 8.5 %copy-start.6 = (s32[3]{0:T(128)S(1)}, s32[3]{0:T(128)}, u32[]{:S(2)}) copy-start(s32[3]{0:T(128)} %param.59) | copy-start | bytes 40
  7.5 200.4 %collective-permute-start.45 = (bf16[4,32,1024]{2,1,0:T(8,128)(2,1)S(1)}, bf16[4,32,1024]{2,1,0:T(8,128)(2,1)S(1)}, u32[]{:S(2)}, u32[]{:S(2)}) collective-permute-start(bf16[4,32,1024]{2,1,0:T(8,128)(2,1)S(1)} %bitcast.92), channel_id=1, source_target_pairs={{1,0},{0,1},{3,2},{2,3},{5,4},{4,5},{7,6},{6,7},{9,8},{8,9},{11,10... | collective-permute-start | bytes 786440 | tf_op jit(solution)/shard_map/ppermute | solution.py:89
  9.5 199.6 %collective-permute-start.46 = (bf16[4,32,1024]{2,1,0:T(8,128)(2,1)S(1)}, bf16[4,32,1024]{2,1,0:T(8,128)(2,1)S(1)}, u32[]{:S(2)}, u32[]{:S(2)}) collective-permute-start(bf16[4,32,1024]{2,1,0:T(8,128)(2,1)S(1)} %bitcast.93), channel_id=1, source_target_pairs={{2,0},{3,1},{4,2},{5,3},{6,4},{7,5},{0,6},{1,7},{10,8},{11,9},{12,... | collective-permute-start | bytes 786440 | tf_op jit(solution)/shard_map/ppermute | solution.py:89
  12.3 197.4 %collective-permute-start.47 = (bf16[4,32,1024]{2,1,0:T(8,128)(2,1)S(1)}, bf16[4,32,1024]{2,1,0:T(8,128)(2,1)S(1)}, u32[]{:S(2)}, u32[]{:S(2)}) collective-permute-start(bf16[4,32,1024]{2,1,0:T(8,128)(2,1)S(1)} %bitcast.94), channel_id=1, source_target_pairs={{3,0},{2,1},{5,2},{4,3},{7,4},{6,5},{1,6},{0,7},{11,8},{10,9},{13,... | collective-permute-start | bytes 786440 | tf_op jit(solution)/shard_map/ppermute | solution.py:89
  12.7 197.1 %collective-permute-start.48 = (bf16[4,32,1024]{2,1,0:T(8,128)(2,1)S(1)}, bf16[4,32,1024]{2,1,0:T(8,128)(2,1)S(1)}, u32[]{:S(2)}, u32[]{:S(2)}) collective-permute-start(bf16[4,32,1024]{2,1,0:T(8,128)(2,1)S(1)} %bitcast.95), channel_id=1, source_target_pairs={{4,0},{5,1},{6,2},{7,3},{0,4},{1,5},{2,6},{3,7},{12,8},{13,9},{14,... | collective-permute-start | bytes 786440 | tf_op jit(solution)/shard_map/ppermute | solution.py:89
  19.6 48.0 %collective-permute-start.4 = (bf16[2,4,128,1024]{3,2,1,0:T(8,128)(2,1)S(1)}, bf16[2,4,128,1024]{3,2,1,0:T(8,128)(2,1)}, u32[]{:S(2)}, u32[]{:S(2)}) collective-permute-start(bf16[2,4,128,1024]{3,2,1,0:T(8,128)(2,1)S(1)} %param.4), channel_id=1, source_target_pairs={{0,40},{8,32},{16,56},{24,48},{32,8},{40,0},{48,24},{56,16},{64,10... | collective-permute-start | bytes 6291464 | tf_op jit(solution)/shard_map/cond/branch_4_fun/ppermute | solution.py:96
  78.9 50.0 %collective-permute-start.16 = (bf16[2,4,128,1024]{3,2,1,0:T(8,128)(2,1)S(1)}, bf16[2,4,128,1024]{3,2,1,0:T(8,128)(2,1)}, u32[]{:S(2)}, u32[]{:S(2)}) collective-permute-start(bf16[2,4,128,1024]{3,2,1,0:T(8,128)(2,1)S(1)} %param.16), channel_id=1, source_target_pairs={{0,16},{8,24},{16,0},{24,8},{32,48},{40,56},{48,32},{56,40},{64,80... | collective-permute-start | bytes 6291464 | tf_op jit(solution)/shard_map/cond/branch_1_fun/ppermute | solution.py:96
  137.2 47.3 %collective-permute-start.33 = (bf16[2,4,128,1024]{3,2,1,0:T(8,128)(2,1)S(1)}, bf16[2,4,128,1024]{3,2,1,0:T(8,128)(2,1)}, u32[]{:S(2)}, u32[]{:S(2)}) collective-permute-start(bf16[2,4,128,1024]{3,2,1,0:T(8,128)(2,1)S(1)} %param.33), channel_id=1, source_target_pairs={{0,32},{8,40},{16,48},{24,56},{32,0},{40,8},{48,16},{56,24},{64,96... | collective-permute-start | bytes 6291464 | tf_op jit(solution)/shard_map/cond/branch_3_fun/ppermute | solution.py:96
  184.5 25.3 %collective-permute-start.49 = (bf16[4,32,1024]{2,1,0:T(8,128)(2,1)S(1)}, bf16[4,32,1024]{2,1,0:T(8,128)(2,1)}, u32[]{:S(2)}, u32[]{:S(2)}) collective-permute-start(bf16[4,32,1024]{2,1,0:T(8,128)(2,1)S(1)} %bitcast.96), channel_id=1, source_target_pairs={{5,0},{4,1},{7,2},{6,3},{1,4},{0,5},{3,6},{2,7},{13,8},{12,9},{15,... | collective-permute-start | bytes 786440 | tf_op jit(solution)/shard_map/ppermute | solution.py:89
  194.0 4.6 %copy-start.3 = (bf16[1,4,4,1024]{3,2,1,0:T(4,128)(2,1)S(1)}, bf16[1,4,4,1024]{3,2,1,0:T(4,128)(2,1)}, u32[]{:S(2)}) copy-start(bf16[1,4,4,1024]{3,2,1,0:T(4,128)(2,1)} %param.57) | copy-start | bytes 98308
  194.0 5.3 %copy-start.4 = (bf16[1,4,4,1024]{3,2,1,0:T(4,128)(2,1)S(1)}, bf16[1,4,4,1024]{3,2,1,0:T(4,128)(2,1)}, u32[]{:S(2)}) copy-start(bf16[1,4,4,1024]{3,2,1,0:T(4,128)(2,1)} %param.58) | copy-start | bytes 98308
  207.9 10.4 %collective-permute-start.50 = (bf16[4,32,1024]{2,1,0:T(8,128)(2,1)S(1)}, bf16[4,32,1024]{2,1,0:T(8,128)(2,1)S(1)}, u32[]{:S(2)}, u32[]{:S(2)}) collective-permute-start(bf16[4,32,1024]{2,1,0:T(8,128)(2,1)S(1)} %bitcast.97), channel_id=1, source_target_pairs={{6,0},{7,1},{0,2},{1,3},{2,4},{3,5},{4,6},{5,7},{14,8},{15,9},{8,1... | collective-permute-start | bytes 786440 | tf_op jit(solution)/shard_map/ppermute | solution.py:89
  209.2 12.7 %collective-permute-start.51 = (bf16[4,32,1024]{2,1,0:T(8,128)(2,1)S(1)}, bf16[4,32,1024]{2,1,0:T(8,128)(2,1)S(1)}, u32[]{:S(2)}, u32[]{:S(2)}) collective-permute-start(bf16[4,32,1024]{2,1,0:T(8,128)(2,1)S(1)} %bitcast.98), channel_id=1, source_target_pairs={{7,0},{6,1},{1,2},{0,3},{3,4},{2,5},{5,6},{4,7},{15,8},{14,9},{9,1... | collective-permute-start | bytes 786440 | tf_op jit(solution)/shard_map/ppermute | solution.py:89
  221.9 1.4 copy-start.1
